TPU v7x, 128 devices: a whole 4x4x4 slice. The times are simulated.
128 devices in a mesh: row: 8 (over y_lo, x), col: 16 (over z, y_hi, core).
Axes of the slice: x: 4, y: 4 (y_hi: 2, y_lo: 2; y = y_hi * 2 + y_lo), z: 4, core: 2. Of those that a mesh axis runs over, the one named last changes fastest.
Arguments:
- points: bfloat16 [64, 65536], P(None, ('row', 'col')), may hold values from -6 to 6
- solution: float32 [16, 65536], P(None, ('row', 'col')), may hold values from -6 to 6
- residual: float32 [16, 65536], P(None, ('row', 'col')), may hold values from -6 to 6
- direction: float32 [16, 65536], P(None, ('row', 'col')), may hold values from -6 to 6
Outputs:
- solution_next: float32 [16, 65536], P(None, ('row', 'col'))
- residual_next: float32 [16, 65536], P(None, ('row', 'col'))
- direction_next: float32 [16, 65536], P(None, ('row', 'col'))
All inputs are finite; a program needn't handle non-finite values.
Results may differ from a plain program's by a relative error of at most 0.0042.
Values may be sent and summed in bfloat16 or wider, within the bound.
A program may use at most 64 MiB of HBM per device.

v0:
```python
import jax
import jax.numpy as jnp
import numpy as np
from jax import lax
from jax.sharding import PartitionSpec as P

F = 64
TILE = 2048


def pair_table(tile_count, device_count):
    pairs = [(i, j) for i in range(tile_count) for j in range(i, tile_count)]
    slot_count = (len(pairs) + device_count - 1) // device_count
    table = np.full((device_count, slot_count, 2), tile_count, np.int32)
    for position, pair in enumerate(pairs):
        table[position % device_count, position // device_count, 0] = pair[0]
        table[position % device_count, position // device_count, 1] = pair[1]
    return table


def add_columns(accumulated, column_start, piece):
    current = lax.dynamic_slice_in_dim(accumulated, column_start, piece.shape[1], 1)
    return lax.dynamic_update_slice_in_dim(accumulated, current + piece, column_start, 1)


def triangle_terms(everyone, sq_norms, all_directions, my_pairs):
    total_points = everyone.shape[1]
    tile_count = total_points // TILE
    block_rows = min(512, TILE)

    def one_pair(slot_index, accumulated):
        row_tile = my_pairs[slot_index, 0]
        col_tile = my_pairs[slot_index, 1]
        slot_live = row_tile < tile_count
        weight = slot_live.astype(jnp.float32)
        mirror = weight * (row_tile != col_tile).astype(jnp.float32)
        row_base = (jnp.minimum(row_tile, tile_count - 1) * TILE).astype(jnp.int32)
        col_start = (jnp.minimum(col_tile, tile_count - 1) * TILE).astype(jnp.int32)
        col_points = lax.dynamic_slice_in_dim(everyone, col_start, TILE, 1)
        col_norms = lax.dynamic_slice_in_dim(sq_norms, col_start, TILE, 0)
        col_vectors = lax.dynamic_slice_in_dim(all_directions, col_start, TILE, 1)
        mirrored = jnp.zeros((all_directions.shape[0], TILE), jnp.float32)
        for piece_index in range(TILE // block_rows):
            row_start = row_base + piece_index * block_rows
            row_points = lax.dynamic_slice_in_dim(everyone, row_start, block_rows, 1)
            row_norms = lax.dynamic_slice_in_dim(sq_norms, row_start, block_rows, 0)
            row_vectors = lax.dynamic_slice_in_dim(all_directions, row_start, block_rows, 1)
            cross_terms = lax.dot_general(
                row_points, col_points, (((0,), (0,)), ((), ())), preferred_element_type=jnp.float32
            )
            dist = row_norms[:, None] + col_norms[None, :] - 2.0 * cross_terms
            kernel = jnp.exp(-(2.0 / F) * dist).astype(jnp.bfloat16)
            row_terms = lax.dot_general(
                col_vectors, kernel, (((1,), (1,)), ((), ())), preferred_element_type=jnp.float32
            )
            accumulated = add_columns(accumulated, row_start, weight * row_terms)
            mirrored = mirrored + jnp.dot(row_vectors, kernel, preferred_element_type=jnp.float32)
        return add_columns(accumulated, col_start, mirror * mirrored)

    return lax.fori_loop(
        0,
        my_pairs.shape[0],
        one_pair,
        jnp.zeros((all_directions.shape[0], total_points), jnp.float32),
    )


def on_device(points, solution, residual, direction):
    local_width = points.shape[1]
    everyone = lax.all_gather(points, ("row", "col"), axis=1, tiled=True)
    total_points = everyone.shape[1]
    tile_count = total_points // TILE
    sq_norms = jnp.sum(jnp.square(everyone.astype(jnp.float32)), axis=0)
    all_directions = lax.all_gather(
        direction.astype(jnp.bfloat16), ("row", "col"), axis=1, tiled=True
    )
    table = jnp.asarray(pair_table(tile_count, lax.axis_size(("row", "col"))))
    my_pairs = table[lax.axis_index(("row", "col"))]
    accumulated = triangle_terms(everyone, sq_norms, all_directions, my_pairs)
    summed = lax.psum(accumulated, ("row", "col"))
    own_start = lax.axis_index(("row", "col")) * local_width
    own_rows = lax.dynamic_slice_in_dim(summed, own_start, local_width, 1)
    image_rows = 1.0 * direction + own_rows
    old_norm = lax.psum(jnp.sum(residual * residual, axis=1), ("row", "col"))
    curvature = lax.psum(jnp.sum(direction * image_rows, axis=1), ("row", "col"))
    step_size = old_norm / curvature
    residual_next = residual - step_size[:, None] * image_rows
    new_norm = lax.psum(jnp.sum(residual_next * residual_next, axis=1), ("row", "col"))
    solution_next = solution + step_size[:, None] * direction
    direction_next = residual_next + (new_norm / old_norm)[:, None] * direction
    return (solution_next, residual_next, direction_next)


def solution(mesh):
    placed = (
        P(None, ("row", "col")),
        P(None, ("row", "col")),
        P(None, ("row", "col")),
        P(None, ("row", "col")),
    )
    return jax.shard_map(
        on_device,
        mesh=mesh,
        in_specs=placed,
        out_specs=(P(None, ("row", "col")), P(None, ("row", "col")), P(None, ("row", "col"))),
        check_vma=False,
    )
```

profile of v0, /device:TPU:1, one launch (start us, length us, event | category | flops | bytes accessed | tf_op | source)
XLA Modules:
  0.0 835.4 jit_solution(7481728378052199383)
XLA Ops:
  10.1 204.3 %all-gather.5.cloned.1.call-done = bf16[64,65536]{1,0:T(8,128)(2,1)} async-done(((bf16[64,512]{1,0:T(8,128)(2,1)}), bf16[64,65536]{1,0:T(8,128)(2,1)}) %all-gather.5.cloned.1.call-update) | async-done | bytes 8388624 | tf_op jit(solution)/shard_map/all_gather | solution.py:70
  214.4 5.5 multiply_reduce_fusion
  219.9 191.2 %all-gather.3.cloned.1.call-done = bf16[16,65536]{1,0:T(8,128)(2,1)} async-done(((bf16[16,512]{1,0:T(8,128)(2,1)}), bf16[16,65536]{1,0:T(8,128)(2,1)}) %all-gather.3.cloned.1.call-update) | async-done | bytes 2097168 | tf_op jit(solution)/shard_map/all_gather | solution.py:74
  411.0 2.2 broadcast_in_dim.24
  413.3 131.7 %while.15 = (s32[]{:T(128)}, f32[16,65536]{1,0:T(8,128)}, s32[5,2]{0,1:T(2,128)S(1)}, bf16[16,65536]{1,0:T(8,128)(2,1)}, f32[65536]{0:T(1024)S(1)}, /*index=5*/b...) while((s32[]{:T(128)}, f32[16,65536]{1,0:T(8,128)}, ...), condition=%wide.region_4.0_spmd, body=%wide.region_3.0_spmd.sunk | while | flops 826507264 | bytes 28191316 | solution.py:60
  417.3 2.1 exponential_convert_fusion.8
  422.6 2.1 exponential_convert_fusion.9
  428.0 2.1 exponential_convert_fusion.10
  433.4 2.1 exponential_convert_fusion.11
  443.6 2.1 exponential_convert_fusion.8
  448.9 2.1 exponential_convert_fusion.9
  454.3 2.1 exponential_convert_fusion.10
  457.6 2.1 fusion.107
  459.7 2.1 exponential_convert_fusion.11
  469.9 2.1 exponential_convert_fusion.8
  473.1 2.1 fusion.105
  475.2 2.1 exponential_convert_fusion.9
  480.6 2.1 exponential_convert_fusion.10
  486.0 2.1 exponential_convert_fusion.11
  488.1 2.1 fusion.108
  496.2 2.1 exponential_convert_fusion.8
  501.6 2.1 exponential_convert_fusion.9
  506.9 2.1 exponential_convert_fusion.10
  512.3 2.1 exponential_convert_fusion.11
  522.4 2.2 exponential_convert_fusion.8
  527.9 2.2 exponential_convert_fusion.9
  533.3 2.2 exponential_convert_fusion.10
  538.7 2.2 exponential_convert_fusion.11
  540.9 2.1 fusion.108
  545.8 152.4 %all-reduce.3.cloned.1.call-done = f32[16,65536]{1,0:T(8,128)} async-done(((f32[16,65536]{1,0:T(8,128)}), f32[16,65536]{1,0:T(8,128)}) %all-reduce.3.cloned.1.call-update) | async-done | bytes 4194320 | tf_op jit(solution)/shard_map/psum | solution.py:80
  699.1 64.0 %all-reduce = (f32[16]{0:T(128)S(1)}, f32[16]{0:T(128)S(1)}) all-reduce(f32[16]{0:T(128)S(1)} %multiply_reduce_fusion.3, f32[16]{0:T(128)S(1)} %multiply_reduce_fusion.2), channel_id=1, replica_groups=mesh['row'=8,'col'=16] {'row','col'}, use_global_device_ids=true, to_apply=%region_1.0 | all-reduce | flops 32 | bytes 256 | tf_op jit(solution)/shard_map/psum | solution.py:84
  764.6 63.5 %psum.31 = f32[16]{0:T(128)S(1)} all-reduce(f32[16]{0:T(128)S(1)} %get-tuple-element.174), channel_id=1, replica_groups=mesh['row'=8,'col'=16] {'row','col'}, use_global_device_ids=true, to_apply=%region_9.0 | all-reduce | flops 16 | bytes 128 | tf_op jit(solution)/shard_map/psum | solution.py:88
  (73 shorter events, 70.7 us)
Async XLA Ops:
  7.2 207.2 %all-gather.5.cloned.1.call-start = ((), (), s32[]{:S(2)}) async-start(), calls=%async_computation.1 | async-start | bytes 8454144 | tf_op jit(solution)/shard_map/all_gather | solution.py:70
  7.9 403.1 %all-gather.3.cloned.1.call-start = ((), (), s32[]{:S(2)}) async-start(), calls=%async_computation | async-start | bytes 2113536 | tf_op jit(solution)/shard_map/all_gather | solution.py:74
  9.3 688.9 %all-reduce.3.cloned.1.call-start = ((), (), s32[]{:S(2)}) async-start(), calls=%async_computation.2 | async-start | bytes 8388608 | tf_op jit(solution)/shard_map/psum | solution.py:80
  545.0 0.8 copy-start.2
  545.0 153.2 %copy-start = (f32[16,512]{1,0:T(8,128)S(1)}, f32[16,512]{1,0:T(8,128)}, u32[]{:S(2)}) copy-start(f32[16,512]{1,0:T(8,128)} %param.10) | copy-start | bytes 98308
  545.0 218.1 %copy-start.3 = (f32[16,512]{1,0:T(8,128)S(1)}, f32[16,512]{1,0:T(8,128)}, u32[]{:S(2)}) copy-start(f32[16,512]{1,0:T(8,128)} %param.8) | copy-start | bytes 98308
  764.6 64.2 %copy-start.1 = (f32[16,512]{1,0:T(8,128)}, f32[16,512]{1,0:T(8,128)S(1)}, u32[]{:S(2)}) copy-start(f32[16,512]{1,0:T(8,128)S(1)} %get-tuple-element.175) | copy-start | bytes 98308
Sparse Core Ops, SparseCore 0:
  9.7 204.6 all-gather.4
  216.7 194.2 all-gather.2
  545.1 153.0 all-reduce.2
where the time goes:
time: 838 us; the launch traced here: 835 us
  waiting for transfers between devices  549 us (66%)
  blocking collectives  128 us (15%)
  matrix products  112 us (13%)
  loops' own time  16.6 us (2%)
  between operations  13.8 us (2%)
  other arithmetic  10.1 us (1%)
    all_gather x1, waiting for transfers between devices, on_device(): everyone = lax.all_gather(points, ('row', 'col'), axis=1, tiled=True)  204 us
    all_gather x1, waiting for transfers between devices, on_device(): lax.all_gather(direction.astype(jnp.bfloat16), ('row', 'col'), axis=1, ti...  191 us
    psum x1, waiting for transfers between devices, on_device(): summed = lax.psum(accumulated, ('row', 'col'))  152 us
    psum x1, blocking collectives, on_device(): old_norm = lax.psum(jnp.sum(residual * residual, axis=1), ('row', 'col'))  64 us
    psum x1, blocking collectives, on_device(): lax.psum(jnp.sum(residual_next * residual_next, axis=1), ('row', 'col'))  63.5 us
    dot_general x20, matrix products, one_pair(): lax.dot_general(row_points, col_points, (((0,), (0,)), ((), ())), preferr...  42.8 us
    dot_general x20, matrix products, one_pair(): lax.dot_general(col_vectors, kernel, (((1,), (1,)), ((), ())), preferred_...  42.4 us
    dot_general x20, matrix products, one_pair(): jnp.dot(row_vectors, kernel, preferred_element_type=jnp.float32)  26.5 us
  transfers between devices with their start and end apart: 3, of which 3 were waited for; matrix products, arithmetic and copies ran while one was open for 1% of the time, Pallas kernels for 0%

commit v1 on v0

--- a/solution.py
+++ b/solution.py
@@ -81,7 +81,9 @@
     own_start = lax.axis_index(("row", "col")) * local_width
     own_rows = lax.dynamic_slice_in_dim(summed, own_start, local_width, 1)
     image_rows = 1.0 * direction + own_rows
-    old_norm = lax.psum(jnp.sum(residual * residual, axis=1), ("row", "col"))
+    old_norm = jnp.sum(residual * residual, axis=1)
+    for ix in ("row", "col"):
+        old_norm = lax.psum(old_norm, axis_name=ix)
     curvature = lax.psum(jnp.sum(direction * image_rows, axis=1), ("row", "col"))
     step_size = old_norm / curvature
     residual_next = residual - step_size[:, None] * image_rows

time: 838 us -> 874 us (1.043)
  blocking collectives: 128 us -> 177 us
  waiting for transfers between devices: 549 us -> 534 us
    psum x1 -> x3, blocking collectives: 64 us -> 113 us  [the longest x1 65.1 us: on_device(): lax.psum(jnp.sum(direction * image_rows, axis=1), ('row', 'col'))]
    psum x1, waiting for transfers between devices: 152 us -> 138 us  [on_device(): summed = lax.psum(accumulated, ('row', 'col'))]
where the time goes in v1:
time: 874 us; the launch traced here: 871 us
  waiting for transfers between devices  534 us (61%)
  blocking collectives  177 us (20%)
  matrix products  112 us (13%)
  loops' own time  16.6 us (2%)
  between operations  13.8 us (2%)
  other arithmetic  10.1 us (1%)
    all_gather x1, waiting for transfers between devices, on_device(): everyone = lax.all_gather(points, ('row', 'col'), axis=1, tiled=True)  204 us
    all_gather x1, waiting for transfers between devices, on_device(): lax.all_gather(direction.astype(jnp.bfloat16), ('row', 'col'), axis=1, ti...  191 us
    psum x1, waiting for transfers between devices, on_device(): summed = lax.psum(accumulated, ('row', 'col'))  138 us
    psum x1, blocking collectives, on_device(): lax.psum(jnp.sum(direction * image_rows, axis=1), ('row', 'col'))  65.1 us
    psum x1, blocking collectives, on_device(): lax.psum(jnp.sum(residual_next * residual_next, axis=1), ('row', 'col'))  64.5 us
    psum x2, blocking collectives, on_device(): old_norm = lax.psum(old_norm, axis_name=ix)  47.7 us
    dot_general x20, matrix products, one_pair(): lax.dot_general(row_points, col_points, (((0,), (0,)), ((), ())), preferr...  42.8 us
    dot_general x20, matrix products, one_pair(): lax.dot_general(col_vectors, kernel, (((1,), (1,)), ((), ())), preferred_...  42.4 us
  transfers between devices with their start and end apart: 3, of which 3 were waited for; matrix products, arithmetic and copies ran while one was open for 1% of the time, Pallas kernels for 0%

profile of v1, /device:TPU:1, one launch (start us, length us, event | category | flops | bytes accessed | tf_op | source)
XLA Modules:
  0.0 870.7 jit_solution(10551778308989431752)
XLA Ops:
  10.1 204.3 %all-gather.5.cloned.1.call-done = bf16[64,65536]{1,0:T(8,128)(2,1)} async-done(((bf16[64,512]{1,0:T(8,128)(2,1)}), bf16[64,65536]{1,0:T(8,128)(2,1)}) %all-gather.5.cloned.1.call-update) | async-done | bytes 8388624 | tf_op jit(solution)/shard_map/all_gather | solution.py:70
  214.4 5.5 multiply_reduce_fusion
  219.9 191.2 %all-gather.3.cloned.1.call-done = bf16[16,65536]{1,0:T(8,128)(2,1)} async-done(((bf16[16,512]{1,0:T(8,128)(2,1)}), bf16[16,65536]{1,0:T(8,128)(2,1)}) %all-gather.3.cloned.1.call-update) | async-done | bytes 2097168 | tf_op jit(solution)/shard_map/all_gather | solution.py:74
  411.0 2.2 broadcast_in_dim.24
  413.3 131.7 %while.15 = (s32[]{:T(128)}, f32[16,65536]{1,0:T(8,128)}, s32[5,2]{0,1:T(2,128)S(1)}, bf16[16,65536]{1,0:T(8,128)(2,1)}, f32[65536]{0:T(1024)S(1)}, /*index=5*/b...) while((s32[]{:T(128)}, f32[16,65536]{1,0:T(8,128)}, ...), condition=%wide.region_5.0_spmd, body=%wide.region_4.0_spmd.sunk | while | flops 826507264 | bytes 28191316 | solution.py:60
  417.3 2.1 exponential_convert_fusion.8
  422.6 2.1 exponential_convert_fusion.9
  428.0 2.1 exponential_convert_fusion.10
  433.4 2.1 exponential_convert_fusion.11
  443.6 2.1 exponential_convert_fusion.8
  448.9 2.1 exponential_convert_fusion.9
  454.3 2.1 exponential_convert_fusion.10
  457.6 2.1 fusion.107
  459.7 2.1 exponential_convert_fusion.11
  469.9 2.1 exponential_convert_fusion.8
  475.2 2.1 exponential_convert_fusion.9
  480.6 2.1 exponential_convert_fusion.10
  486.0 2.1 exponential_convert_fusion.11
  496.2 2.1 exponential_convert_fusion.8
  501.6 2.1 exponential_convert_fusion.9
  506.9 2.1 exponential_convert_fusion.10
  512.3 2.1 exponential_convert_fusion.11
  522.4 2.2 exponential_convert_fusion.8
  527.9 2.2 exponential_convert_fusion.9
  533.3 2.2 exponential_convert_fusion.10
  538.7 2.2 exponential_convert_fusion.11
  540.9 2.1 fusion.108
  545.8 14.4 %psum.35 = f32[16]{0:T(128)S(1)} all-reduce(f32[16]{0:T(128)S(1)} %multiply_reduce_fusion.3), channel_id=1, replica_groups=mesh['row'=8,'col'=16] {'row'}, use_global_device_ids=true, to_apply=%region_1.0 | all-reduce | flops 16 | bytes 128 | tf_op jit(solution)/shard_map/psum | solution.py:86
  560.2 138.0 %all-reduce.2.cloned.1.call-done = f32[16,65536]{1,0:T(8,128)} async-done(((f32[16,65536]{1,0:T(8,128)}), f32[16,65536]{1,0:T(8,128)}) %all-reduce.2.cloned.1.call-update) | async-done | bytes 4194320 | tf_op jit(solution)/shard_map/psum | solution.py:80
  699.1 33.3 %psum.36 = f32[16]{0:T(128)S(1)} all-reduce(f32[16]{0:T(128)S(1)} %psum.35), channel_id=1, replica_groups=mesh['row'=8,'col'=16] {'col'}, use_global_device_ids=true, to_apply=%region_2.0 | all-reduce | flops 16 | bytes 128 | tf_op jit(solution)/shard_map/psum | solution.py:86
  732.3 65.1 %psum.38 = f32[16]{0:T(128)S(1)} all-reduce(f32[16]{0:T(128)S(1)} %multiply_reduce_fusion.2), channel_id=1, replica_groups=mesh['row'=8,'col'=16] {'row','col'}, use_global_device_ids=true, to_apply=%region_8.0 | all-reduce | flops 16 | bytes 128 | tf_op jit(solution)/shard_map/psum | solution.py:87
  799.0 64.5 %psum.39 = f32[16]{0:T(128)S(1)} all-reduce(f32[16]{0:T(128)S(1)} %get-tuple-element.172), channel_id=1, replica_groups=mesh['row'=8,'col'=16] {'row','col'}, use_global_device_ids=true, to_apply=%region_10.0 | all-reduce | flops 16 | bytes 128 | tf_op jit(solution)/shard_map/psum | solution.py:90
  (75 shorter events, 74.9 us)
Async XLA Ops:
  7.2 207.2 %all-gather.5.cloned.1.call-start = ((), (), s32[]{:S(2)}) async-start(), calls=%async_computation.1 | async-start | bytes 8454144 | tf_op jit(solution)/shard_map/all_gather | solution.py:70
  7.9 403.1 %all-gather.3.cloned.1.call-start = ((), (), s32[]{:S(2)}) async-start(), calls=%async_computation | async-start | bytes 2113536 | tf_op jit(solution)/shard_map/all_gather | solution.py:74
  9.3 688.9 %all-reduce.2.cloned.1.call-start = ((), (), s32[]{:S(2)}) async-start(), calls=%async_computation.2 | async-start | bytes 8388608 | tf_op jit(solution)/shard_map/psum | solution.py:80
  545.0 0.8 copy-start.2
  545.0 153.2 %copy-start = (f32[16,512]{1,0:T(8,128)S(1)}, f32[16,512]{1,0:T(8,128)}, u32[]{:S(2)}) copy-start(f32[16,512]{1,0:T(8,128)} %param.10) | copy-start | bytes 98308
  545.0 252.4 %copy-start.3 = (f32[16,512]{1,0:T(8,128)S(1)}, f32[16,512]{1,0:T(8,128)}, u32[]{:S(2)}) copy-start(f32[16,512]{1,0:T(8,128)} %param.8) | copy-start | bytes 98308
  799.0 65.2 %copy-start.1 = (f32[16,512]{1,0:T(8,128)}, f32[16,512]{1,0:T(8,128)S(1)}, u32[]{:S(2)}) copy-start(f32[16,512]{1,0:T(8,128)S(1)} %get-tuple-element.173) | copy-start | bytes 98308
Sparse Core Ops, SparseCore 0:
  9.7 204.6 all-gather.4
  216.7 194.2 all-gather.2
  545.1 153.0 all-reduce.1

commit v2 on v0

--- a/solution.py
+++ b/solution.py
@@ -67,7 +67,10 @@
 
 def on_device(points, solution, residual, direction):
     local_width = points.shape[1]
-    everyone = lax.all_gather(points, ("row", "col"), axis=1, tiled=True)
+    devices = lax.axis_size(("row", "col"))
+    pieces = jnp.stack([points for _ in range(devices)])
+    pieces = lax.all_to_all(pieces, ("row", "col"), split_axis=0, concat_axis=0)
+    everyone = jnp.concatenate(pieces, axis=1)
     total_points = everyone.shape[1]
     tile_count = total_points // TILE
     sq_norms = jnp.sum(jnp.square(everyone.astype(jnp.float32)), axis=0)

time: 838 us -> 723 us (0.86)
  waiting for transfers between devices: 549 us -> 408 us
  local copies, waits for them, and re-layouts: 7.1 us -> 19.7 us
  starting transfers between devices: 0.12 us -> 12 us
    all_gather x1 -> x0, waiting for transfers between devices: 204 us -> none  [on_device(): everyone = lax.all_gather(points, ('row', 'col'), axis=1, tiled=True)]
    all_to_all x0 -> x1, waiting for transfers between devices: none -> 108 us  [on_device(): pieces = lax.all_to_all(pieces, ('row', 'col'), split_axis=0, concat_axis=0)]
    all_gather x1, waiting for transfers between devices: 191 us -> 148 us  [on_device(): lax.all_gather(direction.astype(jnp.bfloat16), ('row', 'col'), axis=1, ti...]
    all_to_all x0 -> x1, starting transfers between devices: none -> 11.9 us  [on_device(): pieces = lax.all_to_all(pieces, ('row', 'col'), split_axis=0, concat_axis=0)]
  transfers between devices with their start and end apart: 3 -> 3, of which waited for: 3 -> 3; matrix products, arithmetic and copies ran while one was open for 1% -> 2% of each run, Pallas kernels for 0% -> 0%
where the time goes in v2:
time: 723 us; the launch traced here: 720 us
  waiting for transfers between devices  408 us (56%)
  blocking collectives  128 us (18%)
  matrix products  112 us (15%)
  local copies, waits for them, and re-layouts  19.7 us (3%)
  loops' own time  16.6 us (2%)
  between operations  14.1 us (2%)
  starting transfers between devices  12 us (2%)
  other arithmetic  10.3 us (1%)
    psum x1, waiting for transfers between devices, on_device(): summed = lax.psum(accumulated, ('row', 'col'))  152 us
    all_gather x1, waiting for transfers between devices, on_device(): lax.all_gather(direction.astype(jnp.bfloat16), ('row', 'col'), axis=1, ti...  148 us
    all_to_all x1, waiting for transfers between devices, on_device(): pieces = lax.all_to_all(pieces, ('row', 'col'), split_axis=0, concat_axis=0)  108 us
    psum x1, blocking collectives, on_device(): old_norm = lax.psum(jnp.sum(residual * residual, axis=1), ('row', 'col'))  64 us
    psum x1, blocking collectives, on_device(): lax.psum(jnp.sum(residual_next * residual_next, axis=1), ('row', 'col'))  63.5 us
    dot_general x20, matrix products, one_pair(): lax.dot_general(row_points, col_points, (((0,), (0,)), ((), ())), preferr...  43.1 us
    dot_general x20, matrix products, one_pair(): lax.dot_general(col_vectors, kernel, (((1,), (1,)), ((), ())), preferred_...  42.3 us
    dot_general x20, matrix products, one_pair(): jnp.dot(row_vectors, kernel, preferred_element_type=jnp.float32)  26.5 us
  transfers between devices with their start and end apart: 3, of which 3 were waited for; matrix products, arithmetic and copies ran while one was open for 2% of the time, Pallas kernels for 0%

profile of v2, /device:TPU:1, one launch (start us, length us, event | category | flops | bytes accessed | tf_op | source)
XLA Modules:
  0.0 719.8 jit_solution(15552554246238078453)
XLA Ops:
  7.2 5.1 stack.2
  12.3 11.9 %all-to-all-start = ((bf16[128,64,512]{2,1,0:T(8,128)(2,1)}), bf16[128,64,512]{2,1,0:T(8,128)(2,1)}, u32[]{:S(2)}, u32[]{:S(2)}) async-start(bf16[128,64,512]{2,1,0:T(8,128)(2,1)} %stack.2), calls=%async_computation | async-start | bytes 16777216 | tf_op jit(solution)/shard_map/all_to_all | solution.py:72
  25.7 107.5 %all-to-all-done = bf16[128,64,512]{2,1,0:T(8,128)(2,1)} async-done(((bf16[128,64,512]{2,1,0:T(8,128)(2,1)}), bf16[128,64,512]{2,1,0:T(8,128)(2,1)}, u32[]{:S(2)}, u32[]{:S(2)}) %all-to-all-start) | async-done | bytes 8388640 | tf_op jit(solution)/shard_map/all_to_all | solution.py:72
  133.2 6.4 multiply_reduce_fusion
  139.7 7.4 %copy.9 = bf16[128,8,8,512]{3,2,0,1:T(8,128)(2,1)} copy(bf16[128,8,8,512]{3,2,1,0:T(8,128)(2,1)} %bitcast.6) | data formatting | bytes 16777216 | tf_op jit(solution)/shard_map/reshape | solution.py:73
  147.1 147.7 %all-gather.2.cloned.1.call-done = bf16[16,65536]{1,0:T(8,128)(2,1)} async-done(((bf16[16,512]{1,0:T(8,128)(2,1)}), bf16[16,65536]{1,0:T(8,128)(2,1)}) %all-gather.2.cloned.1.call-update) | async-done | bytes 2097168 | tf_op jit(solution)/shard_map/all_gather | solution.py:77
  294.8 2.2 broadcast_in_dim.24
  297.1 131.9 %while.15 = (s32[]{:T(128)}, f32[16,65536]{1,0:T(8,128)}, s32[5,2]{0,1:T(2,128)S(1)}, bf16[16,65536]{1,0:T(8,128)(2,1)}, f32[65536]{0:T(1024)S(1)}, /*index=5*/b...) while((s32[]{:T(128)}, f32[16,65536]{1,0:T(8,128)}, ...), condition=%wide.region_4.0_spmd, body=%wide.region_3.0_spmd.sunk | while | flops 826507264 | bytes 28191316 | solution.py:60
  301.1 2.1 exponential_convert_fusion.8
  306.4 2.1 exponential_convert_fusion.9
  311.8 2.1 exponential_convert_fusion.10
  317.2 2.1 exponential_convert_fusion.11
  327.4 2.1 exponential_convert_fusion.8
  332.8 2.1 exponential_convert_fusion.9
  338.2 2.1 exponential_convert_fusion.10
  341.4 2.1 fusion.107
  343.6 2.1 exponential_convert_fusion.11
  353.7 2.1 exponential_convert_fusion.8
  359.1 2.1 exponential_convert_fusion.9
  364.5 2.1 exponential_convert_fusion.10
  369.9 2.1 exponential_convert_fusion.11
  380.1 2.1 exponential_convert_fusion.8
  385.5 2.1 exponential_convert_fusion.9
  390.9 2.1 exponential_convert_fusion.10
  396.2 2.1 exponential_convert_fusion.11
  406.4 2.2 exponential_convert_fusion.8
  411.8 2.2 exponential_convert_fusion.9
  417.3 2.2 exponential_convert_fusion.10
  422.7 2.2 exponential_convert_fusion.11
  429.9 152.4 %all-reduce.3.cloned.1.call-done = f32[16,65536]{1,0:T(8,128)} async-done(((f32[16,65536]{1,0:T(8,128)}), f32[16,65536]{1,0:T(8,128)}) %all-reduce.3.cloned.1.call-update) | async-done | bytes 4194320 | tf_op jit(solution)/shard_map/psum | solution.py:83
  583.2 64.0 %all-reduce = (f32[16]{0:T(128)S(1)}, f32[16]{0:T(128)S(1)}) all-reduce(f32[16]{0:T(128)S(1)} %multiply_reduce_fusion.3, f32[16]{0:T(128)S(1)} %multiply_reduce_fusion.2), channel_id=1, replica_groups=mesh['row'=8,'col'=16] {'row','col'}, use_global_device_ids=true, to_apply=%region_1.0 | all-reduce | flops 32 | bytes 256 | tf_op jit(solution)/shard_map/psum | solution.py:87
  648.7 63.5 %psum.31 = f32[16]{0:T(128)S(1)} all-reduce(f32[16]{0:T(128)S(1)} %get-tuple-element.174), channel_id=1, replica_groups=mesh['row'=8,'col'=16] {'row','col'}, use_global_device_ids=true, to_apply=%region_9.0 | all-reduce | flops 16 | bytes 128 | tf_op jit(solution)/shard_map/psum | solution.py:91
  (75 shorter events, 75.6 us)
Async XLA Ops:
  12.3 12.0 %copy-start = (f32[16,512]{1,0:T(8,128)S(1)}, f32[16,512]{1,0:T(8,128)}, u32[]{:S(2)}) copy-start(f32[16,512]{1,0:T(8,128)} %param.10) | copy-start | bytes 98308
  12.3 120.9 %all-to-all-start = ((bf16[128,64,512]{2,1,0:T(8,128)(2,1)}), bf16[128,64,512]{2,1,0:T(8,128)(2,1)}, u32[]{:S(2)}, u32[]{:S(2)}) async-start(bf16[128,64,512]{2,1,0:T(8,128)(2,1)} %stack.2), calls=%async_computation | async-start | bytes 16777216 | tf_op jit(solution)/shard_map/all_to_all | solution.py:72
  24.2 270.6 %all-gather.2.cloned.1.call-start = ((), (), s32[]{:S(2)}) async-start(), calls=%async_computation.1 | async-start | bytes 2113536 | tf_op jit(solution)/shard_map/all_gather | solution.py:77
  25.0 557.3 %all-reduce.3.cloned.1.call-start = ((), (), s32[]{:S(2)}) async-start(), calls=%async_computation.2 | async-start | bytes 8388608 | tf_op jit(solution)/shard_map/psum | solution.py:83
  429.0 0.8 copy-start.2
  429.0 218.2 %copy-start.3 = (f32[16,512]{1,0:T(8,128)S(1)}, f32[16,512]{1,0:T(8,128)}, u32[]{:S(2)}) copy-start(f32[16,512]{1,0:T(8,128)} %param.8) | copy-start | bytes 98308
  648.7 64.2 %copy-start.1 = (f32[16,512]{1,0:T(8,128)}, f32[16,512]{1,0:T(8,128)S(1)}, u32[]{:S(2)}) copy-start(f32[16,512]{1,0:T(8,128)S(1)} %get-tuple-element.175) | copy-start | bytes 98308
Sparse Core Ops, SparseCore 0:
  27.3 267.4 all-gather.1
  429.1 153.1 all-reduce.2
